TPU v7x, 256 devices: a whole 4x4x8 slice. The times are simulated.
256 devices in a mesh: pole: 2 (over core), row: 4 (over y), col: 2 (over x_hi), layer: 16 (over z, x_lo).
Axes of the slice: x: 4 (x_hi: 2, x_lo: 2; x = x_hi * 2 + x_lo), y: 4, z: 8, core: 2. Of those that a mesh axis runs over, the one named last changes fastest.
Arguments:
- hamilton: bfloat16 [4096, 4096], P('layer', ('row', 'col')), may hold values from -0.0014648438 to 0.0014648438
- intersection: bfloat16 [4096, 4096], P('layer', ('row', 'col')), may hold values from -0.0014648438 to 0.0014648438
- guess: bfloat16 [2, 2, 4096, 4096], P('pole', None, 'layer', ('row', 'col')), may hold values from -6 to 6
- poles: float32 [2, 2], P('pole'), may hold values from -1.5 to 1.5
- weights: float32 [2, 2], P('pole'), may hold values from -1 to 1
- keep: int32 [2, 32, 32], P('pole'), may hold values from 0 to 1, as said below
Outputs:
- density: float32 [16, 2, 128, 4096], P('layer', 'pole', None, ('row', 'col'))
Inputs may be any that keep to these rules, and one draw needn't show every extreme that they name: keep[p, i, j] is 1 where tile (i, j) survives pole p's filter and 0 where it is dropped; diagonal tiles are always kept.
All inputs are finite; a program needn't handle non-finite values.
Results may differ from a plain program's by a relative error of at most 0.0032.
Values may be sent and summed in bfloat16 or wider, within the bound.
No kernel may reach another device: no remote copies, remote signals or barrier semaphores. Data moves between devices by JAX's collectives and lax.ppermute only.
A program may use at most 64 MiB of HBM per device.

v0:
```python
import jax
import jax.numpy as jnp
from jax import lax
from jax.sharding import Mesh
from jax.sharding import PartitionSpec as P

BLOCK = 128
LAYER = ("layer_0", "layer_1")


def sent_together(arrays, axis, dim, along):
    both = jnp.concatenate(arrays, axis=along)
    whole, at, gathered = (lax.all_gather(both, axis, axis=dim, tiled=True), 0, [])
    for a in arrays:
        gathered.append(lax.slice_in_dim(whole, at, at + a.shape[along], axis=along))
        at += a.shape[along]
    return tuple(gathered)


def whole_of(shard, axes, dim):
    for axis in reversed(axes):
        shard = lax.all_gather(shard, axis, axis=dim, tiled=True)
    return shard


def in_blocks(shard, dim, count):
    lengths = shard.shape
    parts = shard.reshape(*lengths[:dim], count, lengths[dim] // count, *lengths[dim + 1 :])
    return jnp.moveaxis(parts, dim, 0)


def sum_at_owner(shard, axis, dim):
    count = lax.axis_size(axis)
    parts = lax.all_to_all(in_blocks(shard, dim, count), axis, 0, 0, tiled=True)
    return jnp.sum(parts, axis=0)


def tile_mask(keep_float, row_ids, col_ids):
    tile_count = keep_float.shape[0]
    tile_ids = jnp.arange(tile_count, dtype=jnp.int32)
    pick_rows = (row_ids[:, None] // BLOCK == tile_ids[None, :]).astype(jnp.float32)
    pick_cols = (col_ids[:, None] // BLOCK == tile_ids[None, :]).astype(jnp.float32)
    half_mask = jnp.dot(pick_rows, keep_float, precision=lax.Precision.HIGHEST)
    return jnp.dot(half_mask, pick_cols.T, precision=lax.Precision.HIGHEST)


def fold_terms(left_panel, piece):
    real_part = jnp.dot(left_panel[0], piece[0], preferred_element_type=jnp.float32) - jnp.dot(
        left_panel[1], piece[1], preferred_element_type=jnp.float32
    )
    imag_part = jnp.dot(left_panel[0], piece[1], preferred_element_type=jnp.float32) + jnp.dot(
        left_panel[1], piece[0], preferred_element_type=jnp.float32
    )
    return jnp.stack([real_part, imag_part])


def per_device(hamilton, intersection, guess, poles, weights, keep):
    rows_local, cols_local = hamilton.shape
    layer_index = lax.axis_index(LAYER)
    span_index = lax.axis_index("row") * lax.axis_size("col") + lax.axis_index("col")
    row_ids = layer_index * rows_local + jnp.arange(rows_local, dtype=jnp.int32)
    col_ids = span_index * cols_local + jnp.arange(cols_local, dtype=jnp.int32)
    ham_rows, ovl_rows = sent_together((hamilton, intersection), ("row", "col"), 1, 0)
    ham_wide = ham_rows.astype(jnp.float32)
    ovl_wide = ovl_rows.astype(jnp.float32)
    real_pole = poles[0, 0]
    imag_pole = poles[0, 1]
    system_panel = jnp.stack([real_pole * ovl_wide - ham_wide, imag_pole * ovl_wide]).astype(
        jnp.bfloat16
    )
    guess_local = guess[0]
    own_mask = tile_mask(keep[0].astype(jnp.float32), row_ids, col_ids)
    first = fold_terms(system_panel, whole_of(guess_local, LAYER, 1))
    product_local = (own_mask[None] * first).astype(jnp.bfloat16)
    guess_panel = lax.all_gather(guess_local, ("row", "col"), axis=2, tiled=True)
    back = fold_terms(guess_panel, lax.all_gather(product_local, LAYER, axis=1, tiled=True))
    refined = own_mask[None] * (2.0 * guess_local.astype(jnp.float32) - back)
    contrib = weights[0, 0] * refined[0] - weights[0, 1] * refined[1]
    reduced = sum_at_owner(contrib, "pole", 0)
    return reduced.reshape(1, 1, reduced.shape[0], cols_local)


def solution(mesh):
    split = Mesh(
        mesh.devices.reshape(mesh.shape["pole"], mesh.shape["row"], mesh.shape["col"], 8, 2),
        ("pole", "row", "col", "layer_0", "layer_1"),
    )
    return jax.shard_map(
        per_device,
        mesh=split,
        in_specs=(
            P(LAYER, ("row", "col")),
            P(LAYER, ("row", "col")),
            P("pole", None, LAYER, ("row", "col")),
            P("pole", None),
            P("pole", None),
            P("pole", None, None),
        ),
        out_specs=P(LAYER, "pole", None, ("row", "col")),
        check_vma=False,
    )
```

profile of v0, /device:TPU:1, one launch (start us, length us, event | category | flops | bytes accessed | tf_op | source)
XLA Modules:
  0.0 499.8 jit_solution(3519931919193923435)
XLA Ops:
  6.5 0.7 all-gather.13.cloned.1.call-update
  7.3 0.0 all-gather.9.cloned.1.call-start
  7.3 1.9 pad_maximum_fusion
  9.2 0.0 all-gather.9.cloned.1.call-update
  9.2 0.0 all-gather.15.cloned.1.call-start
  9.3 29.9 %all-gather.13.cloned.1.call-done = bf16[1,2,512,512]{3,2,1,0:T(8,128)(2,1)} async-done(((bf16[1,2,256,512]{3,2,1,0:T(8,128)(2,1)}), bf16[1,2,512,512]{3,2,1,0:T(8,128)(2,1)}) %all-gather.13.cloned.1.call-update) | async-done | bytes 1048592 | tf_op jit(solution)/shard_map/all_gather | solution.py:22
  39.2 0.0 all-gather.17.cloned.1.call-start
  39.2 0.5 all-gather.17.cloned.1.call-update
  39.7 0.0 all-gather.11.cloned.1.call-start
  39.8 1.4 fusion.40
  41.2 1.0 fusion.30
  42.2 0.5 fusion.28
  42.7 77.4 %all-gather.9.cloned.1.call-done = bf16[512,4096]{1,0:T(8,128)(2,1)} async-done(((bf16[512,512]{1,0:T(8,128)(2,1)}), bf16[512,4096]{1,0:T(8,128)(2,1)}) %all-gather.9.cloned.1.call-update) | async-done | bytes 4194320 | tf_op jit(solution)/shard_map/all_gather | solution.py:13
  120.1 94.4 %all-gather.15.cloned.1.call-done = bf16[1,2,4096,512]{3,2,1,0:T(8,128)(2,1)} async-done(((bf16[1,2,512,512]{3,2,1,0:T(8,128)(2,1)}), bf16[1,2,4096,512]{3,2,1,0:T(8,128)(2,1)}) %all-gather.15.cloned.1.call-update) | async-done | bytes 8388624 | tf_op jit(solution)/shard_map/all_gather | solution.py:22
  214.5 5.0 %fusion.3 = f32[256,512]{1,0:T(8,128)S(1)} fusion(bf16[1,2,4096,512]{3,2,1,0:T(8,128)(2,1)} %all-gather.15.cloned.1.call-done, f32[]{:T(128)} %bitcast.5, bf16[512,4096]{1,0:T(8,128)(2,1)} %all-gather.9.cloned.1.call-done), kind=kOutput, calls=%fused_computation.9 | convolution fusion | flops 1076887552 | bytes 6816256 | tf_op jit(solution)/shard_map/dot_general | solution.py:51
  219.5 0.2 copy-done.2
  219.7 4.5 fusion.4
  224.2 1.9 fusion.20
  226.1 1.9 fusion.24
  228.1 1.0 fusion.25
  229.1 0.6 fusion.39
  229.8 63.1 %all-gather.17.cloned.1.call-done = bf16[1,2,256,4096]{3,2,1,0:T(8,128)(2,1)} async-done(((bf16[1,2,256,512]{3,2,1,0:T(8,128)(2,1)}), bf16[1,2,256,4096]{3,2,1,0:T(8,128)(2,1)}) %all-gather.17.cloned.1.call-update) | async-done | bytes 4194320 | tf_op jit(solution)/shard_map/all_gather | solution.py:75
  292.9 182.6 %all-gather.11.cloned.1.call-done = bf16[2,4096,512]{2,1,0:T(8,128)(2,1)} async-done(((bf16[2,256,512]{2,1,0:T(8,128)(2,1)}), bf16[2,4096,512]{2,1,0:T(8,128)(2,1)}) %all-gather.11.cloned.1.call-update) | async-done | bytes 8388624 | tf_op jit(solution)/shard_map/all_gather | solution.py:76
  475.5 4.2 fusion.7
  479.7 1.0 copy-done.3
  480.7 3.0 fusion.8
  483.7 1.2 fusion.16
  485.0 1.2 fusion.14
  486.3 0.2 fusion.26
  486.5 1.4 fusion.27
  487.9 4.6 all_to_all.5
  492.6 0.7 reduce_sum.9
  (15 shorter events, 0.1 us)
Async XLA Ops:
  6.5 32.6 %all-gather.13.cloned.1.call-start = ((), (), s32[]{:S(2)}) async-start(), calls=%async_computation.3 | async-start | bytes 1572864 | tf_op jit(solution)/shard_map/all_gather | solution.py:22
  7.3 112.8 %all-gather.9.cloned.1.call-start = ((), (), s32[]{:S(2)}) async-start(), calls=%async_computation.1 | async-start | bytes 4718592 | tf_op jit(solution)/shard_map/all_gather | solution.py:13
  9.2 205.3 %all-gather.15.cloned.1.call-start = ((), (), s32[]{:S(2)}) async-start(), calls=%async_computation.4 | async-start | bytes 9437184 | tf_op jit(solution)/shard_map/all_gather | solution.py:22
  39.2 253.7 %all-gather.17.cloned.1.call-start = ((), (), s32[]{:S(2)}) async-start(), calls=%async_computation.5 | async-start | bytes 4718592 | tf_op jit(solution)/shard_map/all_gather | solution.py:75
  39.7 435.7 %all-gather.11.cloned.1.call-start = ((), (), s32[]{:S(2)}) async-start(), calls=%async_computation.2 | async-start | bytes 8912896 | tf_op jit(solution)/shard_map/all_gather | solution.py:76
  214.5 5.2 %copy-start.2 = (bf16[1,2,4096,512]{3,2,1,0:T(8,128)(2,1)S(1)}, bf16[1,2,4096,512]{3,2,1,0:T(8,128)(2,1)}, u32[]{:S(2)}) copy-start(bf16[1,2,4096,512]{3,2,1,0:T(8,128)(2,1)} %all-gather.15.cloned.1.call-done) | copy-start | bytes 25165828
  219.7 4.5 copy-start.5
  226.1 3.0 copy-start.1
  475.5 5.2 %copy-start.3 = (bf16[2,4096,512]{2,1,0:T(8,128)(2,1)S(1)}, bf16[2,4096,512]{2,1,0:T(8,128)(2,1)}, u32[]{:S(2)}) copy-start(bf16[2,4096,512]{2,1,0:T(8,128)(2,1)} %all-gather.11.cloned.1.call-done) | copy-start | bytes 25165828
  480.7 3.0 copy-start.4
  485.0 1.3 copy-start
Sparse Core Ops, SparseCore 0:
  9.1 29.9 all-gather.12
  41.6 78.4 all-gather.8
  121.9 92.5 all-gather.14
  216.8 76.0 all-gather.16
  294.5 180.8 all-gather.10
where the time goes:
time: 500 us
  waiting for transfers between devices  449 us (90%)
  matrix products  24.5 us (5%)
  between operations  13.3 us (3%)
  other arithmetic  5.32 us (1%)
    all_gather x1, waiting for transfers between devices, per_device(): lax.all_gather(product_local, LAYER, axis=1, tiled=True)  183 us
    all_gather x2, waiting for transfers between devices, whole_of(): shard = lax.all_gather(shard, axis, axis=dim, tiled=True)  124 us
    all_gather x1, waiting for transfers between devices, sent_together(): lax.all_gather(both, axis, axis=dim, tiled=True)  77.4 us
    all_gather x1, waiting for transfers between devices, per_device(): lax.all_gather(guess_local, ('row', 'col'), axis=2, tiled=True)  63.1 us
  transfers between devices with their start and end apart: 5, of which 5 were waited for; matrix products, arithmetic and copies ran while one was open for 4% of the time, Pallas kernels for 0%

commit v1 on v0

--- a/solution.py
+++ b/solution.py
@@ -73,7 +73,12 @@
     first = fold_terms(system_panel, whole_of(guess_local, LAYER, 1))
     product_local = (own_mask[None] * first).astype(jnp.bfloat16)
     guess_panel = lax.all_gather(guess_local, ("row", "col"), axis=2, tiled=True)
-    back = fold_terms(guess_panel, lax.all_gather(product_local, LAYER, axis=1, tiled=True))
+    back = fold_terms(
+        guess_panel,
+        jnp.concatenate(
+            lax.all_to_all(jnp.stack([product_local] * lax.axis_size(LAYER)), LAYER, 0, 0), axis=1
+        ),
+    )
     refined = own_mask[None] * (2.0 * guess_local.astype(jnp.float32) - back)
     contrib = weights[0, 0] * refined[0] - weights[0, 1] * refined[1]
     reduced = sum_at_owner(contrib, "pole", 0)

time: 500 us -> 459 us (0.918)
  waiting for transfers between devices: 449 us -> 394 us
  local copies, waits for them, and re-layouts: 3.25 us -> 14 us
  starting transfers between devices: 0.16 us -> 5.36 us
    all_to_all x0 -> x1, waiting for transfers between devices: none -> 190 us  [per_device(): lax.all_to_all(jnp.stack([product_local] * lax.axis_size(LAYER)), LAYER,...]
    all_gather x1 -> x0, waiting for transfers between devices: 183 us -> none  [per_device(): lax.all_gather(product_local, LAYER, axis=1, tiled=True)]
    all_gather x1, waiting for transfers between devices: 63.1 us -> 0.01 us  [per_device(): lax.all_gather(guess_local, ('row', 'col'), axis=2, tiled=True)]
    slice x0 -> x1, local copies, waits for them, and re-layouts: none -> 5.81 us  [fold_terms(): piece[0]]
    all_to_all x0 -> x1, starting transfers between devices: none -> 5.23 us  [per_device(): lax.all_to_all(jnp.stack([product_local] * lax.axis_size(LAYER)), LAYER,...]
  transfers between devices with their start and end apart: 5 -> 5, of which waited for: 5 -> 4; matrix products, arithmetic and copies ran while one was open for 4% -> 2% of each run, Pallas kernels for 0% -> 0%
where the time goes in v1:
time: 459 us
  waiting for transfers between devices  394 us (86%)
  matrix products  22.6 us (5%)
  local copies, waits for them, and re-layouts  14 us (3%)
  between operations  13.3 us (3%)
  starting transfers between devices  5.36 us (1%)
  blocking collectives  5.24 us (1%)
    all_to_all x1, waiting for transfers between devices, per_device(): lax.all_to_all(jnp.stack([product_local] * lax.axis_size(LAYER)), LAYER,...  190 us
    all_gather x2, waiting for transfers between devices, whole_of(): shard = lax.all_gather(shard, axis, axis=dim, tiled=True)  124 us
    all_gather x1, waiting for transfers between devices, sent_together(): lax.all_gather(both, axis, axis=dim, tiled=True)  78 us
    dot_general x2, matrix products, fold_terms(): jnp.dot(left_panel[0], piece[0], preferred_element_type=jnp.float32)  10 us
  transfers between devices with their start and end apart: 5, of which 4 were waited for; matrix products, arithmetic and copies ran while one was open for 2% of the time, Pallas kernels for 0%

profile of v1, /device:TPU:1, one launch (start us, length us, event | category | flops | bytes accessed | tf_op | source)
XLA Modules:
  0.0 458.6 jit_solution(951863874355902365)
XLA Ops:
  6.5 0.7 all-gather.10.cloned.1.call-update
  7.3 0.0 all-gather.8.cloned.1.call-start
  7.3 1.9 pad_maximum_fusion
  9.2 0.0 all-gather.12.cloned.1.call-start
  9.2 29.9 %all-gather.10.cloned.1.call-done = bf16[1,2,512,512]{3,2,1,0:T(8,128)(2,1)} async-done(((bf16[1,2,256,512]{3,2,1,0:T(8,128)(2,1)}), bf16[1,2,512,512]{3,2,1,0:T(8,128)(2,1)}) %all-gather.10.cloned.1.call-update) | async-done | bytes 1048592 | tf_op jit(solution)/shard_map/all_gather | solution.py:22
  39.2 1.4 fusion.41
  40.6 1.0 fusion.30
  41.6 0.5 fusion.28
  42.1 78.0 %all-gather.8.cloned.1.call-done = bf16[512,4096]{1,0:T(8,128)(2,1)} async-done(((bf16[512,512]{1,0:T(8,128)(2,1)}), bf16[512,4096]{1,0:T(8,128)(2,1)}) %all-gather.8.cloned.1.call-update) | async-done | bytes 4194320 | tf_op jit(solution)/shard_map/all_gather | solution.py:13
  120.1 94.4 %all-gather.12.cloned.1.call-done = bf16[1,2,4096,512]{3,2,1,0:T(8,128)(2,1)} async-done(((bf16[1,2,512,512]{3,2,1,0:T(8,128)(2,1)}), bf16[1,2,4096,512]{3,2,1,0:T(8,128)(2,1)}) %all-gather.12.cloned.1.call-update) | async-done | bytes 8388624 | tf_op jit(solution)/shard_map/all_gather | solution.py:22
  214.5 5.8 %fusion.4 = f32[256,512]{1,0:T(8,128)S(1)} fusion(bf16[1,2,4096,512]{3,2,1,0:T(8,128)(2,1)} %all-gather.12.cloned.1.call-done, bf16[512,4096]{1,0:T(8,128)(2,1)} %all-gather.8.cloned.1.call-done, f32[]{:T(128)} %bitcast.3), kind=kOutput, calls=%fused_computation.8 | convolution fusion | flops 1078984704 | bytes 8913408 | tf_op jit(solution)/shard_map/dot_general | solution.py:48
  220.3 1.2 copy-done.5
  221.5 1.9 fusion.3
  223.4 1.9 fusion.16
  225.3 1.9 fusion.20
  227.2 0.2 fusion.25
  227.4 4.2 stack.20
  231.6 5.2 %all-to-all-start = ((bf16[16,2,256,512]{3,2,1,0:T(8,128)(2,1)}), bf16[16,2,256,512]{3,2,1,0:T(8,128)(2,1)}, u32[]{:S(2)}, u32[]{:S(2)}) async-start(bf16[16,2,256,512]{3,2,1,0:T(8,128)(2,1)} %stack.20), calls=%async_computation | async-start | bytes 16777216 | tf_op jit(solution)/shard_map/all_to_all | solution.py:79
  236.8 0.0 all-gather.14.cloned.1.call-start
  236.9 0.5 all-gather.14.cloned.1.call-update
  237.4 0.6 fusion.40
  238.0 190.1 %all-to-all-done = bf16[16,2,256,512]{3,2,1,0:T(8,128)(2,1)} async-done(((bf16[16,2,256,512]{3,2,1,0:T(8,128)(2,1)}), bf16[16,2,256,512]{3,2,1,0:T(8,128)(2,1)}, u32[]{:S(2)}, u32[]{:S(2)}) %all-to-all-start) | async-done | bytes 8388640 | tf_op jit(solution)/shard_map/all_to_all | solution.py:79
  428.1 5.8 %fusion.39 = (bf16[1,16,256,512]{3,2,0,1:T(8,128)(2,1)}, bf16[1,16,256,512]{3,2,0,1:T(8,128)(2,1)}) fusion(bf16[2,16,256,512]{3,2,0,1:T(8,128)(2,1)} %bitcast.9), kind=kLoop, calls=%fused_computation.54 | loop fusion | bytes 16777216 | tf_op jit(solution)/shard_map/slice | solution.py:48
  433.9 4.2 fusion.7
  438.1 3.0 fusion.8
  441.1 1.2 fusion.24
  442.4 0.9 copy-done.1
  443.3 1.2 fusion.22
  444.6 0.2 fusion.26
  444.8 1.3 fusion.27
  446.1 5.2 %all_to_all.10 = f32[2,128,512]{2,1,0:T(8,128)S(1)} all-to-all(f32[2,128,512]{2,1,0:T(8,128)S(1)} %bitcast.67), channel_id=1, replica_groups=mesh['pole'=2,'row'=4,'col'=2,'layer_0'=8,'layer_1'=2] {'pole'}, dimensions={0} | all-to-all | bytes 1048576 | tf_op jit(solution)/shard_map/all_to_all | solution.py:34
  451.3 0.7 reduce_sum.9
  (18 shorter events, 0.1 us)
Async XLA Ops:
  6.5 32.6 %all-gather.10.cloned.1.call-start = ((), (), s32[]{:S(2)}) async-start(), calls=%async_computation.3 | async-start | bytes 1572864 | tf_op jit(solution)/shard_map/all_gather | solution.py:22
  7.3 112.8 %all-gather.8.cloned.1.call-start = ((), (), s32[]{:S(2)}) async-start(), calls=%async_computation.2 | async-start | bytes 4718592 | tf_op jit(solution)/shard_map/all_gather | solution.py:13
  9.2 205.3 %all-gather.12.cloned.1.call-start = ((), (), s32[]{:S(2)}) async-start(), calls=%async_computation.4 | async-start | bytes 9437184 | tf_op jit(solution)/shard_map/all_gather | solution.py:22
  214.5 5.9 %copy-start.4 = (bf16[1,2,4096,512]{3,2,1,0:T(8,128)(2,1)S(1)}, bf16[1,2,4096,512]{3,2,1,0:T(8,128)(2,1)}, u32[]{:S(2)}) copy-start(bf16[1,2,4096,512]{3,2,1,0:T(8,128)(2,1)} %all-gather.12.cloned.1.call-done) | copy-start | bytes 25165828
  214.5 7.0 %copy-start.5 = (bf16[512,4096]{1,0:T(8,128)(2,1)S(1)}, bf16[512,4096]{1,0:T(8,128)(2,1)}, u32[]{:S(2)}) copy-start(bf16[512,4096]{1,0:T(8,128)(2,1)} %all-gather.8.cloned.1.call-done) | copy-start | bytes 12582916
  231.6 5.8 %copy-start.3 = (f32[1,2]{1,0:T(1,128)S(1)}, f32[1,2]{1,0:T(1,128)}, u32[]{:S(2)}) copy-start(f32[1,2]{1,0:T(1,128)} %param.10) | copy-start | bytes 28
  231.6 196.5 %all-to-all-start = ((bf16[16,2,256,512]{3,2,1,0:T(8,128)(2,1)}), bf16[16,2,256,512]{3,2,1,0:T(8,128)(2,1)}, u32[]{:S(2)}, u32[]{:S(2)}) async-start(bf16[16,2,256,512]{3,2,1,0:T(8,128)(2,1)} %stack.20), calls=%async_computation | async-start | bytes 16777216 | tf_op jit(solution)/shard_map/all_to_all | solution.py:79
  236.8 197.0 %all-gather.14.cloned.1.call-start = ((), (), s32[]{:S(2)}) async-start(), calls=%async_computation.5 | async-start | bytes 4718592 | tf_op jit(solution)/shard_map/all_gather | solution.py:75
  433.9 4.2 copy-start.2
  438.1 3.0 copy-start.6
  441.1 2.2 copy-start.1
  443.3 1.3 copy-start
Sparse Core Ops, SparseCore 0:
  9.1 29.9 all-gather.9
  41.6 78.4 all-gather.7
  121.9 92.5 all-gather.11
  239.8 79.7 all-gather.13
